TPU v7x, 32 devices: a whole 2x2x4 slice. The times are simulated.
32 devices in a mesh: groups: 2 (over x), kv: 16 (over z, y, core).
Axes of the slice: x: 2, y: 2, z: 4, core: 2. Of those that a mesh axis runs over, the one named last changes fastest.
Arguments:
- queries: bfloat16 [64, 8192], P(('groups', 'kv')), parts along dimension 0, may hold values from -48 to 48
- keys: bfloat16 [16384, 1024], P(('groups', 'kv')), parts along dimension 0, may hold values from -6 to 6
- values: bfloat16 [16384, 1024], P(('groups', 'kv')), parts along dimension 0, may hold values from -6 to 6
- block_live: int32 [32, 128], P('groups', 'kv'), parts along dimension 0, may hold values from 0 to 1, as said below
- span_offset: int32 [2], P('groups'), parts along dimension 0, may hold values from 2048 to 7648
Outputs:
- attended: bfloat16 [64, 8192], P(('groups', 'kv')), parts along dimension 0
There are 2 independent parts, one for each index of `groups`. A program takes and returns all parts, laid end to end along the dimension named above; each array names one. Nothing has to cross between parts.
Inputs may be any that keep to these rules, and one draw needn't show every extreme that they name: `block_live`: column 0 is 1 for every query shard.
All inputs are finite; a program needn't handle non-finite values.
Results may differ from a plain program's by a relative error of at most 0.0018.
Values may be sent and summed in bfloat16 or wider, within the bound.
A program may use at most 128 MiB of HBM per device.

v0:
```python
import functools
import math

import jax
import jax.numpy as jnp
from jax import lax
from jax.experimental import pallas as pl
from jax.experimental.pallas import tpu as pltpu
from jax.sharding import PartitionSpec as P

HD = 128
BLK = 64
SEG = 256
SCORE_FLOOR = -30.0
MASKED = -1e30
STEPS = 32767.0
CHUNKS = 4
STATS = 4
MESH = pl.DeviceIdType.MESH


def flip(index, mask):
    result = index
    bit = 1
    while bit <= mask:
        if mask & bit:
            result = result + bit - 2 * bit * ((index // bit) % 2)
        bit *= 2
    return result


def build_bias(n, tile, q_dev, me, holder, kv_dev, live_ref, offset):
    rows = n * tile
    blocks, shards = live_ref.shape
    live = (live_ref[...] > 0).astype(jnp.float32).astype(jnp.bfloat16)
    row = lax.broadcasted_iota(jnp.int32, (rows, shards), 0)
    col = lax.broadcasted_iota(jnp.int32, (rows, shards), 1)
    pick = ((row // tile) ^ me == col).astype(jnp.float32).astype(jnp.bfloat16)
    spread = lax.broadcasted_iota(jnp.int32, (blocks, kv_dev), 1) // BLK
    spread = (spread == lax.broadcasted_iota(jnp.int32, (blocks, kv_dev), 0)).astype(jnp.float32)
    by_row = lax.dot_general(
        pick, live, (((1,), (1,)), ((), ())), preferred_element_type=jnp.float32
    ).astype(jnp.bfloat16)
    cells = jnp.dot(by_row, spread.astype(jnp.bfloat16), preferred_element_type=jnp.float32)
    position = holder * kv_dev + lax.broadcasted_iota(jnp.int32, (1, kv_dev), 1)
    row1 = lax.broadcasted_iota(jnp.int32, (rows, 1), 0)
    at = offset + ((row1 // tile) ^ me) * q_dev + row1 % q_dev
    allowed = (position <= at) & ((position >= offset) | (cells > 0.5))
    return jnp.where(allowed, 0.0, MASKED)


def kernel(
    n, q_dev, offset_ref, live_hbm, q_hbm, k_hbm, v_hbm, out_ref,
    q_ref, live_ref, qbuf, kbuf, vbuf, lbuf, bias, obuf, rbuf, sbuf, sgot, mdiag, tdiag, adiag,
    kv_sem, in_sem, l_send, l_recv, k_send, k_recv, v_send, v_recv,
    p_send, p_recv, z_send, z_recv, y_send, y_recv, o_send, o_recv, s_send, s_recv,
):
    me = lax.axis_index("kv")
    heads, tile, _ = q_hbm.shape
    kv_dev = k_hbm.shape[0]
    half = heads // 2
    per = half // CHUNKS
    wide = per * HD
    rows = n * tile
    far = n // 4
    core = me % 2
    mate = 1 - core

    def remote(src, dst, send, recv, slot):
        return pltpu.make_async_remote_copy(
            src_ref=src, dst_ref=dst, send_sem=send, recv_sem=recv,
            device_id={"kv": flip(me, slot)}, device_id_type=MESH,
        )

    def columns(side, c):
        return pl.ds(pl.multiple_of(side * (half * HD) + c * wide, HD), wide)

    barrier = pltpu.get_barrier_semaphore()
    near = [s for s in range(1, n) if s % 4 < 2] + [2]
    for s in reversed(near):
        pl.semaphore_signal(
            barrier, inc=1, device_id={"kv": flip(me, s)}, device_id_type=MESH
        )
    q_load = pltpu.make_async_copy(q_hbm, q_ref, in_sem.at[0])
    live_load = pltpu.make_async_copy(live_hbm, live_ref, in_sem.at[1])
    q_load.start()
    live_load.start()
    own = pl.ds(0, kv_dev)
    theirs = pl.ds(kv_dev, kv_dev)
    loads = []
    for c in range(CHUNKS):
        here = pl.ds(c * wide, wide)
        k_load = pltpu.make_async_copy(
            k_hbm.at[:, columns(core, c)], kbuf.at[own, here], kv_sem.at[0, c]
        )
        v_load = pltpu.make_async_copy(
            v_hbm.at[:, columns(core, c)], vbuf.at[own, here], kv_sem.at[1, c]
        )
        k_load.start()
        v_load.start()
        loads.append((k_load, v_load))
    q_load.wait()
    live_load.wait()
    qbuf[:, 0, 0, 0] = q_ref[pl.ds(core * half, half)]
    pl.semaphore_wait(barrier, len(near))

    live_copy = remote(live_ref, lbuf, l_send.at[0], l_recv.at[0], 1)
    mates, swaps, relays = [], [], []
    for c in range(CHUNKS):
        part = pl.ds(c * per, per)
        for hi in reversed(range(1, far)):
            for a in range(2):
                side = core if a == 0 else mate
                remote(
                    q_ref.at[pl.ds(side * half + c * per, per)], qbuf.at[part, hi, 0, a],
                    z_send.at[c], z_recv.at[c], hi * 4 + a,
                ).start()
        copy = remote(
            q_ref.at[pl.ds(mate * half + c * per, per)], qbuf.at[part, 0, 0, 1],
            p_send.at[c], p_recv.at[c], 1,
        )
        copy.start()
        mates.append(copy)
    live_copy.start()
    for c in range(CHUNKS):
        here = pl.ds(c * wide, wide)
        k_swap = remote(
            k_hbm.at[:, columns(mate, c)], kbuf.at[theirs, here], k_send.at[c], k_recv.at[c], 1
        )
        v_swap = remote(
            v_hbm.at[:, columns(mate, c)], vbuf.at[theirs, here], v_send.at[c], v_recv.at[c], 1
        )
        k_swap.start()
        v_swap.start()
        swaps.append((k_swap, v_swap))

    offset = offset_ref[0]
    bias[:, :kv_dev] = build_bias(n, tile, q_dev, me, me, kv_dev, live_ref, offset)
    live_copy.wait()
    bias[:, kv_dev:] = build_bias(n, tile, q_dev, me, flip(me, 1), kv_dev, lbuf, offset)

    for c in range(CHUNKS):
        part = pl.ds(c * per, per)
        mates[c].wait_recv()
        rest = qbuf.at[part, pl.ds(1, far - 1), 0]
        pltpu.make_async_copy(rest, rest, z_recv.at[c]).wait()
        relay = remote(
            qbuf.at[part, :, 0], qbuf.at[part, :, 1], y_send.at[c], y_recv.at[c], 2
        )
        relay.start()
        relays.append(relay)

    score_scale = 1.0 / math.sqrt(HD)
    lane = lax.broadcasted_iota(jnp.int32, (rows, HD), 1)
    row = lax.broadcasted_iota(jnp.int32, (rows, HD), 0) % tile

    for c in range(CHUNKS):
        part = pl.ds(c * per, per)
        for copy in loads[c]:
            copy.wait()
        for copy in swaps[c]:
            copy.wait_recv()
        relays[c].wait_recv()
        for g in range(c * per, (c + 1) * per):
            queries = qbuf[g].reshape(rows, HD)
            cols = slice(g * HD, (g + 1) * HD)
            accs, peaks, totals = [], [], []
            for s in range(2 * kv_dev // SEG):
                keys = slice(s * SEG, (s + 1) * SEG)
                scores = lax.dot_general(
                    queries, kbuf[keys, cols], (((1,), (1,)), ((), ())),
                    preferred_element_type=jnp.float32,
                )
                scores = scores * score_scale + bias[:, keys]
                peak = jnp.maximum(jnp.max(scores, axis=1, keepdims=True), SCORE_FLOOR)
                weights = jnp.exp(scores - peak)
                totals.append(jnp.sum(weights, axis=1, keepdims=True))
                peaks.append(peak)
                accs.append(
                    jnp.dot(
                        weights.astype(jnp.bfloat16), vbuf[keys, cols],
                        preferred_element_type=jnp.float32,
                    )
                )
            peak = functools.reduce(jnp.maximum, peaks)
            scales = [jnp.exp(p - peak) for p in peaks]
            acc = sum(a * e for a, e in zip(accs, scales))
            total = sum(t * e for t, e in zip(totals, scales))
            most = jnp.max(jnp.abs(acc), axis=1, keepdims=True)
            inverse = jnp.where(most > 0.0, 1.0 / most, 0.0)
            coded = jnp.round(acc * inverse * STEPS).astype(jnp.int32).astype(jnp.int16)
            obuf[g] = coded.reshape(n, tile, HD)
            here = lane == g * tile + row
            if g == 0:
                mdiag[...] = jnp.where(here, peak, 0.0)
                tdiag[...] = jnp.where(here, total, 0.0)
                adiag[...] = jnp.where(here, most, 0.0)
            else:
                mdiag[...] = jnp.where(here, peak, mdiag[...])
                tdiag[...] = jnp.where(here, total, tdiag[...])
                adiag[...] = jnp.where(here, most, adiag[...])
        if c == CHUNKS - 1:
            for k, diag in enumerate((mdiag, tdiag, adiag)):
                for s in range(n):
                    line = jnp.sum(diag[s * tile : (s + 1) * tile], axis=0, keepdims=True)
                    if s == 0:
                        sgot[0, 0, k : k + 1] = line
                    else:
                        sbuf[s, k : k + 1] = line
            for s in reversed(range(1, n)):
                remote(sbuf.at[s], sgot.at[s // 2, s % 2], s_send.at[0], s_recv.at[0], s).start()
        for s in reversed(range(1, n)):
            remote(
                obuf.at[part, s], rbuf.at[part, s], o_send.at[c], o_recv.at[c], s
            ).start()

    others = pl.ds(1, n - 1)
    stats_in = sbuf.at[others]
    pltpu.make_async_copy(stats_in, stats_in, s_recv.at[0]).wait()
    weight = []
    for a in range(2):
        peaks = sgot[:, a, 0]
        peak = jnp.max(peaks, axis=0, keepdims=True)
        scale = jnp.exp(peaks - peak)
        total = jnp.sum(scale * sgot[:, a, 1], axis=0, keepdims=True)
        weight.append(jnp.transpose(scale * (sgot[:, a, 2] / total)))
    for c in range(CHUNKS):
        part = pl.ds(c * per, per)
        rest = rbuf.at[part, others]
        pltpu.make_async_copy(rest, rest, o_recv.at[c]).wait()
        for g in range(c * per, (c + 1) * per):
            span = slice(g * tile, (g + 1) * tile)
            for a in range(2):
                acc = None
                for chip in range(n // 2):
                    s = chip * 2 + a
                    block = obuf[g, 0] if s == 0 else rbuf[g, s]
                    term = block.astype(jnp.int32).astype(jnp.float32)
                    term = term * weight[a][span, chip : chip + 1]
                    acc = term if acc is None else acc + term
                side = core if a == 0 else mate
                out_ref[side * half + g] = (acc * (1.0 / STEPS)).astype(jnp.bfloat16)

    for c in range(CHUNKS):
        part = pl.ds(c * per, per)
        mates[c].wait_send()
        rest = qbuf.at[part, pl.ds(1, far - 1), 0]
        pltpu.make_async_copy(rest, rest, z_send.at[c]).wait()
        relays[c].wait_send()
        for copy in swaps[c]:
            copy.wait_send()
        rest = obuf.at[part, others]
        pltpu.make_async_copy(rest, rest, o_send.at[c]).wait()
    pltpu.make_async_copy(stats_in, stats_in, s_send.at[0]).wait()


def on_device(queries, keys, values, block_live, span_offset):
    n = lax.axis_size("kv")
    q_dev, width = queries.shape
    kv_dev, kv_width = keys.shape
    shards, blocks = block_live.shape
    heads = kv_width // HD
    half = heads // 2
    group = width // kv_width
    tile = group * q_dev
    rows = n * tile
    tiles = queries.reshape(q_dev, heads * group, HD).transpose(1, 0, 2).reshape(heads, tile, HD)
    vmem = pl.BlockSpec(memory_space=pltpu.VMEM)
    hbm = pl.BlockSpec(memory_space=pltpu.HBM)
    dma = pltpu.SemaphoreType.DMA
    out = pl.pallas_call(
        functools.partial(kernel, n, q_dev),
        out_shape=jax.ShapeDtypeStruct((heads, tile, HD), jnp.bfloat16),
        in_specs=[pl.BlockSpec(memory_space=pltpu.SMEM), hbm, hbm, hbm, hbm],
        out_specs=vmem,
        scratch_shapes=[
            pltpu.VMEM((heads, tile, HD), jnp.bfloat16),
            pltpu.VMEM((blocks, shards), jnp.int32),
            pltpu.VMEM((half, n // 4, 2, 2, tile, HD), jnp.bfloat16),
            pltpu.VMEM((2 * kv_dev, kv_width // 2), jnp.bfloat16),
            pltpu.VMEM((2 * kv_dev, kv_width // 2), jnp.bfloat16),
            pltpu.VMEM((blocks, shards), jnp.int32),
            pltpu.VMEM((rows, 2 * kv_dev), jnp.float32),
            pltpu.VMEM((half, n, tile, HD), jnp.int16),
            pltpu.VMEM((half, n, tile, HD), jnp.int16),
            pltpu.VMEM((n, STATS, HD), jnp.float32),
            pltpu.VMEM((n // 2, 2, STATS, HD), jnp.float32),
            pltpu.VMEM((rows, HD), jnp.float32),
            pltpu.VMEM((rows, HD), jnp.float32),
            pltpu.VMEM((rows, HD), jnp.float32),
            dma((2, CHUNKS)), dma((2,)), dma((1,)), dma((1,)),
            *[dma((CHUNKS,)) for _ in range(12)],
            dma((1,)), dma((1,)),
        ],
        compiler_params=pltpu.CompilerParams(
            collective_id=0, has_side_effects=True, vmem_limit_bytes=53 * 1024 * 1024
        ),
    )(span_offset, block_live.T, tiles, keys, values)
    return out.reshape(heads * group, q_dev, HD).transpose(1, 0, 2).reshape(q_dev, width)


def solution(mesh):
    placed = (
        P(("groups", "kv"), None),
        P(("groups", "kv"), None),
        P(("groups", "kv"), None),
        P("groups", "kv"),
        P("groups"),
    )
    return jax.shard_map(
        on_device, mesh=mesh, in_specs=placed, out_specs=P(("groups", "kv"), None), check_vma=False
    )
```

profile of v0, /device:TPU:0, one launch (start us, length us, event | category | flops | bytes accessed | tf_op | source)
XLA Modules:
  0.0 24.0 jit_solution(15353420547865796976)
XLA Ops:
  0.0 0.0 copy-start.1
  0.7 0.0 copy-done.1
  0.7 0.0 copy-start
  0.7 0.8 %copy-done = bf16[2,8192]{1,0:T(2,128)(2,1)S(1)} copy-done((bf16[2,8192]{1,0:T(2,128)(2,1)S(1)}, bf16[2,8192]{1,0:T(2,128)(2,1)}, u32[]{:S(2)}) %copy-start) | copy-done | bytes 32792
  1.4 21.9 %shard_map.55 = bf16[8,16,128]{2,1,0:T(8,128)(2,1)S(1)} custom-call(s32[1]{0:T(128)S(6)} %copy.9.offset_ref, s32[8,16]{1,0:T(8,128)S(1)} %bitcast.13, bf16[8,16,128]{2,1,0:T(8,128)(2,1)S(1)} %bitcast.12, bf16[512,1024]{1,0:T(8,128)(2,1)} %k_hbm.1, bf16[512,1024]{1,0:T(8,128)(2,1)} %v_hbm.1), custom_call_target="tpu_custom_call" | custom-call | tf_op jit(solution)/shard_map/pallas_call | solution.py:271
  23.4 0.6 %copy.10 = bf16[2,8192]{1,0:T(2,128)(2,1)} copy(bf16[2,8192]{1,0:T(2,128)(2,1)S(1)} %bitcast.11) | data formatting | bytes 65536
Async XLA Ops:
  0.0 0.7 %copy-start.1 = (s32[16,8]{0,1:T(8,128)S(1)}, s32[16,8]{0,1:T(8,128)}, u32[]{:S(2)}) copy-start(s32[16,8]{0,1:T(8,128)} %param.8) | copy-start | bytes 1540
  0.7 0.8 %copy-start = (bf16[2,8192]{1,0:T(2,128)(2,1)S(1)}, bf16[2,8192]{1,0:T(2,128)(2,1)}, u32[]{:S(2)}) copy-start(bf16[2,8192]{1,0:T(2,128)(2,1)} %param.5) | copy-start | bytes 98308
where the time goes:
time: 24.2 us; the launch traced here: 24 us
  Pallas kernels  21.9 us (90%)
  local copies, waits for them, and re-layouts  1.4 us (6%)
  between operations  0.68 us (3%)
    pallas_call x1, Pallas kernels, on_device(): pl.pallas_call(functools.partial(kernel, n, q_dev), out_shape=jax.ShapeDt...  21.9 us
    unnamed x5, local copies, waits for them, and re-layouts  1.4 us

commit v1 on v0

--- a/solution.py
+++ b/solution.py
@@ -25,6 +25,15 @@
     while bit <= mask:
         if mask & bit:
             result = result + bit - 2 * bit * ((index // bit) % 2)
+        bit *= 2
+    return result
+
+
+def xor(a, b, n):
+    result = 0
+    bit = 1
+    while bit < n:
+        result = result + (a // bit + b // bit) % 2 * bit
         bit *= 2
     return result
 
@@ -53,7 +62,7 @@
     n, q_dev, offset_ref, live_hbm, q_hbm, k_hbm, v_hbm, out_ref,
     q_ref, live_ref, qbuf, kbuf, vbuf, lbuf, bias, obuf, rbuf, sbuf, sgot, mdiag, tdiag, adiag,
     kv_sem, in_sem, l_send, l_recv, k_send, k_recv, v_send, v_recv,
-    p_send, p_recv, z_send, z_recv, y_send, y_recv, o_send, o_recv, s_send, s_recv,
+    q_send, q_recv, o_send, o_recv, s_send, s_recv,
 ):
     me = lax.axis_index("kv")
     heads, tile, _ = q_hbm.shape
@@ -64,6 +73,8 @@
     rows = n * tile
     far = n // 4
     core = me % 2
+    y = me // 2 % 2
+    z = me // 4
     mate = 1 - core
 
     def remote(src, dst, send, recv, slot):
@@ -72,12 +83,30 @@
             device_id={"kv": flip(me, slot)}, device_id_type=MESH,
         )
 
+    def targets(step):
+        found = []
+        for k in range(1, far):
+            to = (z + far + step * k) % far
+            base = xor(z, to, far) * 4
+            for yd in range(2)[::step]:
+                for cd in range(2):
+                    slot = base + (y + yd) % 2 * 2 + (core + cd) % 2
+                    found.append((slot, to * 4 + yd * 2 + cd, cd))
+        for s in (3, 2, 1):
+            found.append((s, flip(me, s), core if s % 2 == 0 else mate))
+        return found
+
+    def push(src, dst, send, recv, device):
+        pltpu.make_async_remote_copy(
+            src_ref=src, dst_ref=dst, send_sem=send, recv_sem=recv,
+            device_id={"kv": device}, device_id_type=MESH,
+        ).start()
+
     def columns(side, c):
         return pl.ds(pl.multiple_of(side * (half * HD) + c * wide, HD), wide)
 
     barrier = pltpu.get_barrier_semaphore()
-    near = [s for s in range(1, n) if s % 4 < 2] + [2]
-    for s in reversed(near):
+    for s in reversed(range(1, n)):
         pl.semaphore_signal(
             barrier, inc=1, device_id={"kv": flip(me, s)}, device_id_type=MESH
         )
@@ -100,27 +129,18 @@
         v_load.start()
         loads.append((k_load, v_load))
     q_load.wait()
-    live_load.wait()
-    qbuf[:, 0, 0, 0] = q_ref[pl.ds(core * half, half)]
-    pl.semaphore_wait(barrier, len(near))
-
-    live_copy = remote(live_ref, lbuf, l_send.at[0], l_recv.at[0], 1)
-    mates, swaps, relays = [], [], []
+    pl.semaphore_wait(barrier, n - 1)
+
+    live_copy = remote(live_hbm, lbuf, l_send.at[0], l_recv.at[0], 1)
+    swaps = []
+    outward = targets(-1)
     for c in range(CHUNKS):
         part = pl.ds(c * per, per)
-        for hi in reversed(range(1, far)):
-            for a in range(2):
-                side = core if a == 0 else mate
-                remote(
-                    q_ref.at[pl.ds(side * half + c * per, per)], qbuf.at[part, hi, 0, a],
-                    z_send.at[c], z_recv.at[c], hi * 4 + a,
-                ).start()
-        copy = remote(
-            q_ref.at[pl.ds(mate * half + c * per, per)], qbuf.at[part, 0, 0, 1],
-            p_send.at[c], p_recv.at[c], 1,
-        )
-        copy.start()
-        mates.append(copy)
+        for slot, device, side in outward:
+            push(
+                q_ref.at[pl.ds(side * half + c * per, per)], qbuf.at[part, slot],
+                q_send.at[c], q_recv.at[c], device,
+            )
     live_copy.start()
     for c in range(CHUNKS):
         here = pl.ds(c * wide, wide)
@@ -134,22 +154,15 @@
         v_swap.start()
         swaps.append((k_swap, v_swap))
 
+    live_load.wait()
+    qbuf[:, 0] = q_ref[pl.ds(core * half, half)]
     offset = offset_ref[0]
     bias[:, :kv_dev] = build_bias(n, tile, q_dev, me, me, kv_dev, live_ref, offset)
     live_copy.wait()
     bias[:, kv_dev:] = build_bias(n, tile, q_dev, me, flip(me, 1), kv_dev, lbuf, offset)
 
-    for c in range(CHUNKS):
-        part = pl.ds(c * per, per)
-        mates[c].wait_recv()
-        rest = qbuf.at[part, pl.ds(1, far - 1), 0]
-        pltpu.make_async_copy(rest, rest, z_recv.at[c]).wait()
-        relay = remote(
-            qbuf.at[part, :, 0], qbuf.at[part, :, 1], y_send.at[c], y_recv.at[c], 2
-        )
-        relay.start()
-        relays.append(relay)
-
+    inward = targets(1)
+    others = pl.ds(1, n - 1)
     score_scale = 1.0 / math.sqrt(HD)
     lane = lax.broadcasted_iota(jnp.int32, (rows, HD), 1)
     row = lax.broadcasted_iota(jnp.int32, (rows, HD), 0) % tile
@@ -160,7 +173,8 @@
             copy.wait()
         for copy in swaps[c]:
             copy.wait_recv()
-        relays[c].wait_recv()
+        rest = qbuf.at[part, others]
+        pltpu.make_async_copy(rest, rest, q_recv.at[c]).wait()
         for g in range(c * per, (c + 1) * per):
             queries = qbuf[g].reshape(rows, HD)
             cols = slice(g * HD, (g + 1) * HD)
@@ -207,14 +221,13 @@
                         sgot[0, 0, k : k + 1] = line
                     else:
                         sbuf[s, k : k + 1] = line
-            for s in reversed(range(1, n)):
-                remote(sbuf.at[s], sgot.at[s // 2, s % 2], s_send.at[0], s_recv.at[0], s).start()
-        for s in reversed(range(1, n)):
-            remote(
-                obuf.at[part, s], rbuf.at[part, s], o_send.at[c], o_recv.at[c], s
-            ).start()
-
-    others = pl.ds(1, n - 1)
+            for slot, device, _ in inward:
+                push(
+                    sbuf.at[slot], sgot.at[slot // 2, slot % 2], s_send.at[0], s_recv.at[0], device
+                )
+        for slot, device, _ in inward:
+            push(obuf.at[part, slot], rbuf.at[part, slot], o_send.at[c], o_recv.at[c], device)
+
     stats_in = sbuf.at[others]
     pltpu.make_async_copy(stats_in, stats_in, s_recv.at[0]).wait()
     weight = []
@@ -243,10 +256,8 @@
 
     for c in range(CHUNKS):
         part = pl.ds(c * per, per)
-        mates[c].wait_send()
-        rest = qbuf.at[part, pl.ds(1, far - 1), 0]
-        pltpu.make_async_copy(rest, rest, z_send.at[c]).wait()
-        relays[c].wait_send()
+        rest = qbuf.at[part, others]
+        pltpu.make_async_copy(rest, rest, q_send.at[c]).wait()
         for copy in swaps[c]:
             copy.wait_send()
         rest = obuf.at[part, others]
@@ -276,7 +287,7 @@
         scratch_shapes=[
             pltpu.VMEM((heads, tile, HD), jnp.bfloat16),
             pltpu.VMEM((blocks, shards), jnp.int32),
-            pltpu.VMEM((half, n // 4, 2, 2, tile, HD), jnp.bfloat16),
+            pltpu.VMEM((half, n, tile, HD), jnp.bfloat16),
             pltpu.VMEM((2 * kv_dev, kv_width // 2), jnp.bfloat16),
             pltpu.VMEM((2 * kv_dev, kv_width // 2), jnp.bfloat16),
             pltpu.VMEM((blocks, shards), jnp.int32),
@@ -289,13 +300,13 @@
             pltpu.VMEM((rows, HD), jnp.float32),
             pltpu.VMEM((rows, HD), jnp.float32),
             dma((2, CHUNKS)), dma((2,)), dma((1,)), dma((1,)),
-            *[dma((CHUNKS,)) for _ in range(12)],
+            *[dma((CHUNKS,)) for _ in range(8)],
             dma((1,)), dma((1,)),
         ],
         compiler_params=pltpu.CompilerParams(
             collective_id=0, has_side_effects=True, vmem_limit_bytes=53 * 1024 * 1024
         ),
-    )(span_offset, block_live.T, tiles, keys, values)
+    )(span_offset, *(pltpu.with_memory_space_constraint(x, pltpu.HBM) for x in (block_live.T, tiles, keys, values)))
     return out.reshape(heads * group, q_dev, HD).transpose(1, 0, 2).reshape(q_dev, width)
 
 

time: 24.2 us -> 22.3 us (0.921)
  Pallas kernels: 21.9 us -> 20.9 us
  local copies, waits for them, and re-layouts: 1.4 us -> 0.62 us
    pallas_call x1, Pallas kernels: 21.9 us -> 20.9 us  [on_device(): pl.pallas_call(functools.partial(kernel, n, q_dev), out_shape=jax.ShapeDt...]
    unnamed x5 -> x1, local copies, waits for them, and re-layouts: 1.4 us -> 0.62 us
where the time goes in v1:
time: 22.3 us; the launch traced here: 22.2 us
  Pallas kernels  20.9 us (94%)
  between operations  0.66 us (3%)
  local copies, waits for them, and re-layouts  0.62 us (3%)
    pallas_call x1, Pallas kernels, on_device(): pl.pallas_call(functools.partial(kernel, n, q_dev), out_shape=jax.ShapeDt...  20.9 us
    unnamed x1, local copies, waits for them, and re-layouts  0.62 us

profile of v1, /device:TPU:0, one launch (start us, length us, event | category | flops | bytes accessed | tf_op | source)
XLA Modules:
  0.0 22.2 jit_solution(3927937820199798640)
XLA Ops:
  0.7 20.9 %shard_map.55 = bf16[8,16,128]{2,1,0:T(8,128)(2,1)S(1)} custom-call(s32[1]{0:T(128)S(6)} %copy.9.offset_ref, s32[8,16]{1,0:T(8,128)} %bitcast.13, bf16[8,16,128]{2,1,0:T(8,128)(2,1)} %bitcast.12, bf16[512,1024]{1,0:T(8,128)(2,1)} %k_hbm.1, bf16[512,1024]{1,0:T(8,128)(2,1)} %v_hbm.1), custom_call_target="tpu_custom_call" | custom-call | tf_op jit(solution)/shard_map/pallas_call | solution.py:282
  21.6 0.6 %copy.10 = bf16[2,8192]{1,0:T(2,128)(2,1)} copy(bf16[2,8192]{1,0:T(2,128)(2,1)S(1)} %bitcast.11) | data formatting | bytes 65536

commit v2 on v1

--- a/solution.py
+++ b/solution.py
@@ -10,12 +10,12 @@
 
 HD = 128
 BLK = 64
-SEG = 256
+LOG2E = math.log2(math.e)
 SCORE_FLOOR = -30.0
 MASKED = -1e30
 STEPS = 32767.0
-CHUNKS = 4
-STATS = 4
+CHUNKS = 2
+SPLIT = 1
 MESH = pl.DeviceIdType.MESH
 
 
@@ -60,7 +60,7 @@
 
 def kernel(
     n, q_dev, offset_ref, live_hbm, q_hbm, k_hbm, v_hbm, out_ref,
-    q_ref, live_ref, qbuf, kbuf, vbuf, lbuf, bias, obuf, rbuf, sbuf, sgot, mdiag, tdiag, adiag,
+    q_ref, live_ref, qbuf, kbuf, vbuf, lbuf, bias, obuf, rbuf, sbuf, sgot, diag,
     kv_sem, in_sem, l_send, l_recv, k_send, k_recv, v_send, v_recv,
     q_send, q_recv, o_send, o_recv, s_send, s_recv,
 ):
@@ -163,9 +163,10 @@
 
     inward = targets(1)
     others = pl.ds(1, n - 1)
-    score_scale = 1.0 / math.sqrt(HD)
-    lane = lax.broadcasted_iota(jnp.int32, (rows, HD), 1)
-    row = lax.broadcasted_iota(jnp.int32, (rows, HD), 0) % tile
+    score_scale = LOG2E / math.sqrt(HD)
+    strip = rows // SPLIT
+    lane = lax.broadcasted_iota(jnp.int32, (strip, HD), 1)
+    row = lax.broadcasted_iota(jnp.int32, (strip, HD), 0) % tile
 
     for c in range(CHUNKS):
         part = pl.ds(c * per, per)
@@ -176,51 +177,42 @@
         rest = qbuf.at[part, others]
         pltpu.make_async_copy(rest, rest, q_recv.at[c]).wait()
         for g in range(c * per, (c + 1) * per):
-            queries = qbuf[g].reshape(rows, HD)
             cols = slice(g * HD, (g + 1) * HD)
-            accs, peaks, totals = [], [], []
-            for s in range(2 * kv_dev // SEG):
-                keys = slice(s * SEG, (s + 1) * SEG)
+            for r in range(SPLIT):
+                mine = slice(r * strip, (r + 1) * strip)
+                slots = slice(r * n // SPLIT, (r + 1) * n // SPLIT)
+                queries = qbuf[g, slots].reshape(strip, HD)
                 scores = lax.dot_general(
-                    queries, kbuf[keys, cols], (((1,), (1,)), ((), ())),
+                    queries, kbuf[:, cols], (((1,), (1,)), ((), ())),
                     preferred_element_type=jnp.float32,
                 )
-                scores = scores * score_scale + bias[:, keys]
-                peak = jnp.maximum(jnp.max(scores, axis=1, keepdims=True), SCORE_FLOOR)
-                weights = jnp.exp(scores - peak)
-                totals.append(jnp.sum(weights, axis=1, keepdims=True))
-                peaks.append(peak)
-                accs.append(
-                    jnp.dot(
-                        weights.astype(jnp.bfloat16), vbuf[keys, cols],
-                        preferred_element_type=jnp.float32,
-                    )
+                scores = scores * score_scale + bias[mine]
+                peak = jnp.max(scores, axis=1, keepdims=True)
+                peak = jnp.maximum(peak, SCORE_FLOOR * LOG2E)
+                weights = jnp.exp2(scores - peak)
+                total = jnp.sum(weights, axis=1, keepdims=True)
+                acc = jnp.dot(
+                    weights.astype(jnp.bfloat16), vbuf[:, cols],
+                    preferred_element_type=jnp.float32,
                 )
-            peak = functools.reduce(jnp.maximum, peaks)
-            scales = [jnp.exp(p - peak) for p in peaks]
-            acc = sum(a * e for a, e in zip(accs, scales))
-            total = sum(t * e for t, e in zip(totals, scales))
-            most = jnp.max(jnp.abs(acc), axis=1, keepdims=True)
-            inverse = jnp.where(most > 0.0, 1.0 / most, 0.0)
-            coded = jnp.round(acc * inverse * STEPS).astype(jnp.int32).astype(jnp.int16)
-            obuf[g] = coded.reshape(n, tile, HD)
-            here = lane == g * tile + row
-            if g == 0:
-                mdiag[...] = jnp.where(here, peak, 0.0)
-                tdiag[...] = jnp.where(here, total, 0.0)
-                adiag[...] = jnp.where(here, most, 0.0)
-            else:
-                mdiag[...] = jnp.where(here, peak, mdiag[...])
-                tdiag[...] = jnp.where(here, total, tdiag[...])
-                adiag[...] = jnp.where(here, most, adiag[...])
+                most = jnp.max(jnp.abs(acc), axis=1, keepdims=True)
+                inverse = jnp.where(most > 0.0, STEPS / most, 0.0)
+                coded = jnp.round(acc * inverse).astype(jnp.int32).astype(jnp.int16)
+                obuf[g, slots] = coded.reshape(n // SPLIT, tile, HD)
+                some = total > 0.0
+                level = jnp.where(some, peak + jnp.log2(total), MASKED)
+                ratio = jnp.where(some, most / total, 0.0)
+                before = 0.0 if g == 0 else diag[mine]
+                here = lane == g * tile + row
+                there = lane == HD // 2 + g * tile + row
+                diag[mine] = jnp.where(here, level, jnp.where(there, ratio, before))
         if c == CHUNKS - 1:
-            for k, diag in enumerate((mdiag, tdiag, adiag)):
-                for s in range(n):
-                    line = jnp.sum(diag[s * tile : (s + 1) * tile], axis=0, keepdims=True)
-                    if s == 0:
-                        sgot[0, 0, k : k + 1] = line
-                    else:
-                        sbuf[s, k : k + 1] = line
+            for s in range(n):
+                line = jnp.sum(diag[s * tile : (s + 1) * tile], axis=0, keepdims=True)
+                if s == 0:
+                    sgot[0, 0] = line
+                else:
+                    sbuf[s] = line
             for slot, device, _ in inward:
                 push(
                     sbuf.at[slot], sgot.at[slot // 2, slot % 2], s_send.at[0], s_recv.at[0], device
@@ -232,11 +224,11 @@
     pltpu.make_async_copy(stats_in, stats_in, s_recv.at[0]).wait()
     weight = []
     for a in range(2):
-        peaks = sgot[:, a, 0]
-        peak = jnp.max(peaks, axis=0, keepdims=True)
-        scale = jnp.exp(peaks - peak)
-        total = jnp.sum(scale * sgot[:, a, 1], axis=0, keepdims=True)
-        weight.append(jnp.transpose(scale * (sgot[:, a, 2] / total)))
+        levels = sgot[:, a, 0]
+        ratios = pltpu.roll(levels, HD // 2, 1)
+        scale = jnp.exp2(levels - jnp.max(levels, axis=0, keepdims=True))
+        total = jnp.sum(scale, axis=0, keepdims=True)
+        weight.append(jnp.transpose(scale * (ratios / total)))
     for c in range(CHUNKS):
         part = pl.ds(c * per, per)
         rest = rbuf.at[part, others]
@@ -275,6 +267,7 @@
     group = width // kv_width
     tile = group * q_dev
     rows = n * tile
+    assert half * tile <= HD // 2
     tiles = queries.reshape(q_dev, heads * group, HD).transpose(1, 0, 2).reshape(heads, tile, HD)
     vmem = pl.BlockSpec(memory_space=pltpu.VMEM)
     hbm = pl.BlockSpec(memory_space=pltpu.HBM)
@@ -294,10 +287,8 @@
             pltpu.VMEM((rows, 2 * kv_dev), jnp.float32),
             pltpu.VMEM((half, n, tile, HD), jnp.int16),
             pltpu.VMEM((half, n, tile, HD), jnp.int16),
-            pltpu.VMEM((n, STATS, HD), jnp.float32),
-            pltpu.VMEM((n // 2, 2, STATS, HD), jnp.float32),
-            pltpu.VMEM((rows, HD), jnp.float32),
-            pltpu.VMEM((rows, HD), jnp.float32),
+            pltpu.VMEM((n, 1, HD), jnp.float32),
+            pltpu.VMEM((n // 2, 2, 1, HD), jnp.float32),
             pltpu.VMEM((rows, HD), jnp.float32),
             dma((2, CHUNKS)), dma((2,)), dma((1,)), dma((1,)),
             *[dma((CHUNKS,)) for _ in range(8)],

time: 22.3 us -> 21.5 us (0.964)
  Pallas kernels: 20.9 us -> 20.1 us
    pallas_call x1, Pallas kernels: 20.9 us -> 20.1 us  [on_device(): pl.pallas_call(functools.partial(kernel, n, q_dev), out_shape=jax.ShapeDt...]
where the time goes in v2:
time: 21.5 us; the launch traced here: 21.4 us
  Pallas kernels  20.1 us (93%)
  between operations  0.66 us (3%)
  local copies, waits for them, and re-layouts  0.62 us (3%)
    pallas_call x1, Pallas kernels, on_device(): pl.pallas_call(functools.partial(kernel, n, q_dev), out_shape=jax.ShapeDt...  20.1 us
    unnamed x1, local copies, waits for them, and re-layouts  0.62 us

profile of v2, /device:TPU:0, one launch (start us, length us, event | category | flops | bytes accessed | tf_op | source)
XLA Modules:
  0.0 21.4 jit_solution(12850286401585323413)
XLA Ops:
  0.7 20.1 %shard_map.55 = bf16[8,16,128]{2,1,0:T(8,128)(2,1)S(1)} custom-call(s32[1]{0:T(128)S(6)} %copy.9.offset_ref, s32[8,16]{1,0:T(8,128)} %bitcast.13, bf16[8,16,128]{2,1,0:T(8,128)(2,1)} %bitcast.12, bf16[512,1024]{1,0:T(8,128)(2,1)} %k_hbm.1, bf16[512,1024]{1,0:T(8,128)(2,1)} %v_hbm.1), custom_call_target="tpu_custom_call" | custom-call | tf_op jit(solution)/shard_map/pallas_call | solution.py:275
  20.7 0.6 %copy.10 = bf16[2,8192]{1,0:T(2,128)(2,1)} copy(bf16[2,8192]{1,0:T(2,128)(2,1)S(1)} %bitcast.11) | data formatting | bytes 65536

commit v3 on v2

--- a/solution.py
+++ b/solution.py
@@ -10,6 +10,7 @@
 
 HD = 128
 BLK = 64
+SEG = 256
 LOG2E = math.log2(math.e)
 SCORE_FLOOR = -30.0
 MASKED = -1e30
@@ -182,19 +183,29 @@
                 mine = slice(r * strip, (r + 1) * strip)
                 slots = slice(r * n // SPLIT, (r + 1) * n // SPLIT)
                 queries = qbuf[g, slots].reshape(strip, HD)
-                scores = lax.dot_general(
-                    queries, kbuf[:, cols], (((1,), (1,)), ((), ())),
-                    preferred_element_type=jnp.float32,
-                )
-                scores = scores * score_scale + bias[mine]
-                peak = jnp.max(scores, axis=1, keepdims=True)
-                peak = jnp.maximum(peak, SCORE_FLOOR * LOG2E)
-                weights = jnp.exp2(scores - peak)
-                total = jnp.sum(weights, axis=1, keepdims=True)
-                acc = jnp.dot(
-                    weights.astype(jnp.bfloat16), vbuf[:, cols],
-                    preferred_element_type=jnp.float32,
-                )
+                accs, peaks, totals = [], [], []
+                for seg in range(2 * kv_dev // SEG):
+                    keys = slice(seg * SEG, (seg + 1) * SEG)
+                    scores = lax.dot_general(
+                        queries, kbuf[keys, cols], (((1,), (1,)), ((), ())),
+                        preferred_element_type=jnp.float32,
+                    )
+                    scores = scores * score_scale + bias[mine, keys]
+                    peak = jnp.max(scores, axis=1, keepdims=True)
+                    peak = jnp.maximum(peak, SCORE_FLOOR * LOG2E)
+                    weights = jnp.exp2(scores - peak)
+                    totals.append(jnp.sum(weights, axis=1, keepdims=True))
+                    peaks.append(peak)
+                    accs.append(
+                        jnp.dot(
+                            weights.astype(jnp.bfloat16), vbuf[keys, cols],
+                            preferred_element_type=jnp.float32,
+                        )
+                    )
+                peak = functools.reduce(jnp.maximum, peaks)
+                scales = [jnp.exp2(p - peak) for p in peaks]
+                acc = sum(a * e for a, e in zip(accs, scales))
+                total = sum(t * e for t, e in zip(totals, scales))
                 most = jnp.max(jnp.abs(acc), axis=1, keepdims=True)
                 inverse = jnp.where(most > 0.0, STEPS / most, 0.0)
                 coded = jnp.round(acc * inverse).astype(jnp.int32).astype(jnp.int16)

time: 21.5 us -> 21.5 us (level)
  no operation moved by 1% of the time
where the time goes in v3:
time: 21.5 us; the launch traced here: 21.3 us
  Pallas kernels  20.1 us (93%)
  between operations  0.66 us (3%)
  local copies, waits for them, and re-layouts  0.62 us (3%)
    pallas_call x1, Pallas kernels, on_device(): pl.pallas_call(functools.partial(kernel, n, q_dev), out_shape=jax.ShapeDt...  20.1 us
    unnamed x1, local copies, waits for them, and re-layouts  0.62 us

profile of v3, /device:TPU:0, one launch (start us, length us, event | category | flops | bytes accessed | tf_op | source)
XLA Modules:
  0.0 21.3 jit_solution(14257374880030332062)
XLA Ops:
  0.7 20.1 %shard_map.55 = bf16[8,16,128]{2,1,0:T(8,128)(2,1)S(1)} custom-call(s32[1]{0:T(128)S(6)} %copy.9.offset_ref, s32[8,16]{1,0:T(8,128)} %bitcast.13, bf16[8,16,128]{2,1,0:T(8,128)(2,1)} %bitcast.12, bf16[512,1024]{1,0:T(8,128)(2,1)} %k_hbm.1, bf16[512,1024]{1,0:T(8,128)(2,1)} %v_hbm.1), custom_call_target="tpu_custom_call" | custom-call | tf_op jit(solution)/shard_map/pallas_call | solution.py:286
  20.7 0.6 %copy.10 = bf16[2,8192]{1,0:T(2,128)(2,1)} copy(bf16[2,8192]{1,0:T(2,128)(2,1)S(1)} %bitcast.11) | data formatting | bytes 65536

commit v4 on v3

--- a/solution.py
+++ b/solution.py
@@ -87,7 +87,10 @@
     def targets(step):
         found = []
         for k in range(1, far):
-            to = (z + far + step * k) % far
+            if step > 0:
+                to = k - 1 + (k - 1 + far - z) // far
+            else:
+                to = (z + far - k) % far
             base = xor(z, to, far) * 4
             for yd in range(2)[::step]:
                 for cd in range(2):
@@ -224,11 +227,11 @@
                     sgot[0, 0] = line
                 else:
                     sbuf[s] = line
-            for slot, device, _ in inward:
+        for slot, device, _ in inward:
+            if c == CHUNKS - 1:
                 push(
                     sbuf.at[slot], sgot.at[slot // 2, slot % 2], s_send.at[0], s_recv.at[0], device
                 )
-        for slot, device, _ in inward:
             push(obuf.at[part, slot], rbuf.at[part, slot], o_send.at[c], o_recv.at[c], device)
 
     stats_in = sbuf.at[others]

time: 21.5 us -> 21.3 us (level)
  no operation moved by 1% of the time
where the time goes in v4:
time: 21.3 us; the launch traced here: 21.2 us
  Pallas kernels  19.9 us (93%)
  between operations  0.66 us (3%)
  local copies, waits for them, and re-layouts  0.62 us (3%)
    pallas_call x1, Pallas kernels, on_device(): pl.pallas_call(functools.partial(kernel, n, q_dev), out_shape=jax.ShapeDt...  19.9 us
    unnamed x1, local copies, waits for them, and re-layouts  0.62 us

profile of v4, /device:TPU:0, one launch (start us, length us, event | category | flops | bytes accessed | tf_op | source)
XLA Modules:
  0.0 21.2 jit_solution(14786232706634713097)
XLA Ops:
  0.7 19.9 %shard_map.55 = bf16[8,16,128]{2,1,0:T(8,128)(2,1)S(1)} custom-call(s32[1]{0:T(128)S(6)} %copy.9.offset_ref, s32[8,16]{1,0:T(8,128)} %bitcast.13, bf16[8,16,128]{2,1,0:T(8,128)(2,1)} %bitcast.12, bf16[512,1024]{1,0:T(8,128)(2,1)} %k_hbm.1, bf16[512,1024]{1,0:T(8,128)(2,1)} %v_hbm.1), custom_call_target="tpu_custom_call" | custom-call | tf_op jit(solution)/shard_map/pallas_call | solution.py:289
  20.6 0.6 %copy.10 = bf16[2,8192]{1,0:T(2,128)(2,1)} copy(bf16[2,8192]{1,0:T(2,128)(2,1)S(1)} %bitcast.11) | data formatting | bytes 65536
